TPU v7x, 32 devices: a whole 2x2x4 slice. The times are simulated.
32 devices in a mesh: row: 8 (over z, y), col: 4 (over x, core).
Axes of the slice: x: 2, y: 2, z: 4, core: 2. Of those that a mesh axis runs over, the one named last changes fastest.
Arguments:
- inputs: bfloat16 [128, 8192], P('row', 'col'), may hold values from -6 to 6
- out_grad: bfloat16 [128, 8192], P('row', 'col'), may hold values from -96 to 96
- gate_weight: bfloat16 [8192, 16384], P('col', 'row'), may hold values from -0.0625 to 0.0625
- up_weight: bfloat16 [8192, 16384], P('col', 'row'), may hold values from -0.0625 to 0.0625
- down_weight: bfloat16 [16384, 8192], P('row', 'col'), may hold values from -0.046875 to 0.046875
Outputs:
- input_grad: bfloat16 [128, 8192], P('row', 'col')
- gate_grad: bfloat16 [8192, 16384], P('col', 'row')
- up_grad: bfloat16 [8192, 16384], P('col', 'row')
- down_grad: bfloat16 [16384, 8192], P('row', 'col')
All inputs are finite; a program needn't handle non-finite values.
Results may differ from a plain program's by a relative error of at most 0.005.
Values may be sent and summed in bfloat16 or wider, within the bound.
No kernel may reach another device: no remote copies, remote signals or barrier semaphores. Data moves between devices by JAX's collectives and lax.ppermute only.
A program may use at most 128 MiB of HBM per device.

v0:
```python
import functools

import jax
import jax.numpy as jnp
from jax import lax
from jax.experimental import pallas as pl
from jax.experimental.pallas import tpu as pltpu
from jax.sharding import PartitionSpec as P


LAYERS = 128
F32 = jnp.float32
BF16 = jnp.bfloat16
VMEM = pl.BlockSpec(memory_space=pltpu.VMEM)
SMEM = pl.BlockSpec(memory_space=pltpu.SMEM)
ANY = pl.BlockSpec(memory_space=pl.ANY)
HBM = pl.BlockSpec(memory_space=pltpu.HBM)
LOAD_LIMIT = 44 << 20


def contract_rows(left, right):
    return lax.dot_general(left, right, (((0,), (0,)), ((), ())), preferred_element_type=F32)


def contract_cols(left, right):
    return lax.dot_general(left, right, (((1,), (1,)), ((), ())), preferred_element_type=F32)


def swap(value, axis, size, mask):
    return lax.ppermute(value, axis, [(i, i ^ mask) for i in range(size)])


def bits_of(size):
    return size.bit_length() - 1


def tiles(total, most):
    size = min(total, most)
    return [pl.ds(start, size) for start in range(0, total, size)]


def cost(flops, arrays):
    moved = sum(a.size * a.dtype.itemsize for a in arrays)
    return pl.CostEstimate(flops=flops, bytes_accessed=moved, transcendentals=0)


def into_kernel(half_ref, tokens_ref, weight_ref, own_ref, other_ref):
    width = own_ref.shape[1]
    for out_ref, half in ((other_ref, 1 - half_ref[0]), (own_ref, half_ref[0])):
        start = pl.multiple_of(half * width, width)
        out_ref[...] = jnp.dot(
            tokens_ref[...], weight_ref[:, pl.ds(start, width)], preferred_element_type=F32
        )


def halves(half_ref, tokens_ref, top_ref, bottom_ref, out_ref):
    width, middle = out_ref.shape[1], top_ref.shape[0]
    columns = pl.ds(pl.multiple_of(half_ref[0] * width, width), width)
    value = jnp.dot(tokens_ref[:, :middle], top_ref[:, columns], preferred_element_type=F32)
    value += jnp.dot(tokens_ref[:, middle:], bottom_ref[:, columns], preferred_element_type=F32)
    out_ref[...] = value


def first_kernel(half_ref, *refs):
    *block_refs, top_ref, bottom_ref, out_ref, tokens_ref = refs
    tokens_ref[...] = jnp.concatenate([ref[...] for ref in block_refs])
    halves(half_ref, tokens_ref, top_ref, bottom_ref, out_ref)


def load_kernel(starts, *refs):
    count = len(starts)
    copies = []
    for k, (start, ref, out_ref) in enumerate(zip(starts, refs, refs[count:])):
        source = ref.at[pl.ds(start, out_ref.shape[0])]
        copies.append(pltpu.make_async_copy(source, out_ref, refs[-1].at[k]))
    for copy in copies:
        copy.start()
    for copy in copies:
        copy.wait()


def load(limit, *spans):
    count = len(spans)
    shapes = tuple(jax.ShapeDtypeStruct((rows, a.shape[1]), a.dtype) for a, _, rows in spans)
    total = sum(shape.size * shape.dtype.itemsize for shape in shapes)
    return pl.pallas_call(
        functools.partial(load_kernel, [start for _, start, _ in spans]),
        out_shape=shapes,
        in_specs=[HBM] * count,
        out_specs=(VMEM,) * count,
        scratch_shapes=[pltpu.SemaphoreType.DMA((count,))],
        cost_estimate=cost(0, shapes),
        compiler_params=pltpu.CompilerParams(vmem_limit_bytes=limit),
    )(*[a for a, _, _ in spans])


def into_half(kernel, half, blocks, *weights):
    count = sum(block.shape[0] for block in blocks)
    shape = jax.ShapeDtypeStruct((count, weights[0].shape[1] // 2), F32)
    tokens = jax.ShapeDtypeStruct((count, blocks[0].shape[1]), BF16)
    shapes = (shape, tokens) if len(blocks) > 1 else (shape,)
    return pl.pallas_call(
        kernel,
        out_shape=shapes,
        in_specs=[SMEM] + [VMEM] * (len(blocks) + 2),
        out_specs=(VMEM,) * len(shapes),
        cost_estimate=cost(2 * count * weights[0].size, [*blocks, *weights, *shapes]),
        compiler_params=pltpu.CompilerParams(vmem_limit_bytes=12 << 20),
    )(half, *blocks, *weights)


def back_kernel(half_ref, tokens_ref, weight_ref, turn_ref, own_ref, other_ref, turned_ref):
    turned_ref[...] = turn_ref[...].T
    width = own_ref.shape[1]
    step = min(width, 512)
    for out_ref, half in ((other_ref, 1 - half_ref[0]), (own_ref, half_ref[0])):
        for at in range(0, width, step):
            start = pl.multiple_of(half * width + at, step)
            value = contract_cols(weight_ref[pl.ds(start, step), :], tokens_ref[...])
            out_ref[:, pl.ds(at, step)] = value.T


def into_hidden(kernel, half, tokens, weight, hidden, *turn):
    shape = jax.ShapeDtypeStruct((tokens.shape[0], hidden // 2), F32)
    turned = [jax.ShapeDtypeStruct(a.shape[::-1], a.dtype) for a in turn]
    return pl.pallas_call(
        kernel,
        out_shape=(shape, shape, *turned),
        in_specs=[SMEM, VMEM, VMEM] + [VMEM] * len(turn),
        out_specs=(VMEM, VMEM) + (VMEM,) * len(turn),
        cost_estimate=cost(2 * tokens.shape[0] * weight.size, [tokens, weight, shape, shape]),
        compiler_params=pltpu.CompilerParams(vmem_limit_bytes=12 << 20),
    )(half, tokens, weight, *turn)


def out_kernel(half_ref, gate_ref, up_ref, top_ref, bottom_ref, up_weight_ref, *rest):
    out_ref = rest[-1]
    width, middle = gate_ref.shape[1], top_ref.shape[0]
    columns = pl.ds(pl.multiple_of(half_ref[0] * width, width), width)
    for part, ref in enumerate((top_ref, bottom_ref)):
        for rows in tiles(middle, 512):
            into = pl.ds(part * middle + rows.start, rows.size)
            value = contract_cols(ref[rows, columns], gate_ref[...])
            value += contract_cols(up_weight_ref[into, columns], up_ref[...])
            value = value.T
            if len(rest) > 1:
                value += rest[0][:, into]
            out_ref[:, into] = value


def out_of_hidden(half, gate, up, top, bottom, up_weight, *total):
    shape = jax.ShapeDtypeStruct((gate.shape[0], up_weight.shape[0]), F32)
    arrays = [gate, up, top, bottom, up_weight, *total]
    return pl.pallas_call(
        out_kernel,
        out_shape=shape,
        in_specs=[SMEM] + [VMEM] * len(arrays),
        out_specs=VMEM,
        cost_estimate=cost(4 * gate.size * up_weight.shape[0], arrays + [shape]),
        compiler_params=pltpu.CompilerParams(vmem_limit_bytes=21 << 20),
    )(half, *arrays)


def write_out(slices, held, sems):
    slots = held.shape[0]
    copies = []
    for step, (make, target) in enumerate(slices):
        slot = step % slots
        if step >= slots:
            copies[step - slots].wait()
        value = make().astype(held.dtype)
        held[slot] = value
        copy = pltpu.make_async_copy(held.at[slot], target, sems.at[slot])
        copy.start()
        copies.append(copy)
    for copy in copies[-slots:]:
        copy.wait()


def down_kernel(scale, half_ref, own_ref, other_ref, grads_ref, out_ref, held, sems):
    rows = held.shape[1]
    width = own_ref.shape[1]
    slices = []
    for ref, half in ((own_ref, half_ref[0]), (other_ref, 1 - half_ref[0])):
        for at in range(0, width, rows):
            make = lambda ref=ref, at=at: scale * contract_rows(ref[:, pl.ds(at, rows)], grads_ref[...])
            start = pl.multiple_of(half * width + at, rows)
            slices.append((make, out_ref.at[pl.ds(start, rows)]))
    write_out(slices, held, sems)


def down_outer(scale, half, own, other, grads):
    tokens, width = own.shape
    features = grads.shape[1]
    rows, slots = min(256, width), 4
    shape = jax.ShapeDtypeStruct((2 * width, features), BF16)
    return pl.pallas_call(
        functools.partial(down_kernel, scale),
        out_shape=shape,
        in_specs=[SMEM, VMEM, VMEM, VMEM],
        out_specs=ANY,
        scratch_shapes=[pltpu.VMEM((slots, rows, features), BF16), pltpu.SemaphoreType.DMA((slots,))],
        cost_estimate=cost(4 * tokens * width * features, [own, other, grads, shape]),
        compiler_params=pltpu.CompilerParams(vmem_limit_bytes=10 << 20),
    )(half, own, other, grads)


def up_kernel(units, count, half_ref, turned_ref, *refs):
    part_refs = refs[: len(units)]
    out_refs, held, sems = refs[-2 - count : -2], refs[-2], refs[-1]
    rows, width = held.shape[1:]
    slices = []
    for (out, own), ref in zip(units, part_refs):
        half = half_ref[0] if own else 1 - half_ref[0]
        columns = pl.ds(pl.multiple_of(half * width, width), width)
        for at in range(0, turned_ref.shape[0], rows):
            make = lambda ref=ref, at=at: jnp.dot(
                turned_ref[pl.ds(at, rows), :], ref[...], preferred_element_type=F32
            )
            slices.append((make, out_refs[out].at[pl.ds(at, rows), columns]))
    write_out(slices, held, sems)


def up_outer(half, turned, parts, begun=None, fresh=0):
    features, _ = turned.shape
    width = parts[0][2].shape[1]
    rows, slots = min(512, features), 4
    shape = jax.ShapeDtypeStruct((features, 2 * width), BF16)
    deltas = [part[2] for part in parts]
    kept = [] if begun is None else [begun]
    outs = len(kept) + fresh
    return pl.pallas_call(
        functools.partial(up_kernel, [part[:2] for part in parts], outs),
        out_shape=(shape,) * outs,
        in_specs=[SMEM] + [VMEM] * (1 + len(deltas)) + [ANY] * len(kept),
        out_specs=(ANY,) * outs,
        scratch_shapes=[pltpu.VMEM((slots, rows, width), BF16), pltpu.SemaphoreType.DMA((slots,))],
        input_output_aliases={2 + len(deltas): 0} if kept else {},
        cost_estimate=cost(2 * turned.size * width * len(deltas), [turned, *deltas, *deltas]),
        compiler_params=pltpu.CompilerParams(vmem_limit_bytes=10 << 20),
    )(half, turned, *deltas, *kept)


def gather(value, near, size, separate):
    for bit in range(3, bits_of(size)):
        value = near = jnp.concatenate([near, swap(value, "row", size, 1 << bit)])
    far = [swap(value, "row", size, 4)]
    if not separate:
        blocks = jnp.concatenate([near] + far)
        blocks = jnp.concatenate([blocks, swap(blocks, "row", size, 2)])
        return [blocks, swap(blocks, "row", size, 1)]
    far += [swap(value, "row", size, 2)]
    near_1 = swap(value, "row", size, 1)
    far += [swap(far[0], "row", size, 2)]
    near_53 = swap(jnp.concatenate(far[:2]), "row", size, 1)
    return [near, *far, near_1, near_53, swap(far[2], "row", size, 1)]


def scatter(value, size):
    def add(kept, sent, mask):
        return kept + swap(sent.astype(BF16), "row", size, mask).astype(F32)

    count = value.shape[0] // 4
    kept, last, sent_kept, sent_last = (value[k * count : (k + 1) * count] for k in range(4))
    last = add(last, sent_last, 1)
    kept = add(kept, sent_kept, 1)
    value = add(kept, last, 2)
    for bit in [2] + list(range(3, bits_of(size)))[::-1]:
        half = value.shape[0] // 2
        value = add(value[:half], value[half:], 1 << bit)
    return value


def feature_sum(parts, size):
    own, other = parts
    total = own + swap(other, "col", size, 1)
    for bit in range(1, bits_of(size)):
        sent = total.astype(BF16)
        total = total + swap(sent, "col", size, 1 << bit).astype(F32)
    return total


def per_device(sizes, inputs, out_grad, gate_weight, up_weight, down_weight):
    mult = (2.0 * LAYERS) ** (-0.5)
    rows, cols = sizes
    hidden_units = gate_weight.shape[1]
    half = (lax.axis_index("col") & 1).astype(jnp.int32).reshape(1)
    own, own_grad = load(1 << 20, (inputs, 0, inputs.shape[0]), (out_grad, 0, out_grad.shape[0]))
    blocks = gather(inputs, own, rows, True)
    grads_all = jnp.concatenate(gather(out_grad, own_grad, rows, False))
    middle = gate_weight.shape[0] // 2
    (gate_top,) = load(LOAD_LIMIT, (gate_weight, 0, middle))
    (gate_bottom,) = load(LOAD_LIMIT, (gate_weight, middle, middle))
    other, tokens_all = into_half(first_kernel, 1 - half, blocks, gate_top, gate_bottom)
    parts = [*into_half(halves, half, [tokens_all], gate_top, gate_bottom), other]
    gate = feature_sum(parts, cols)
    parts = into_hidden(into_kernel, half, tokens_all, up_weight, hidden_units)
    up = feature_sum(parts, cols)
    *parts, tokens_turned = into_hidden(back_kernel, half, grads_all, down_weight, hidden_units, tokens_all)
    back = feature_sum(parts, cols)

    hidden = (gate * jax.nn.sigmoid(gate) * up).astype(BF16)
    hidden_other = swap(hidden, "col", cols, 1)
    down_grad = down_outer(mult, half, hidden, hidden_other, grads_all)

    gate, up, back = lax.optimization_barrier((gate, up, back))
    sig = jax.nn.sigmoid(gate)
    hidden_grad = mult * back
    gate_delta = (hidden_grad * up * sig * (1.0 + gate * (1.0 - sig))).astype(BF16)
    up_delta = (hidden_grad * gate * sig).astype(BF16)
    gate_other = swap(gate_delta, "col", cols, 1)
    up_other = swap(up_delta, "col", cols, 1)

    part = out_of_hidden(half, gate_delta, up_delta, gate_top, gate_bottom, up_weight)
    part = out_of_hidden(1 - half, gate_other, up_other, gate_top, gate_bottom, up_weight, part)
    input_grad = scatter(part, rows).astype(BF16)
    (gate_grad,) = up_outer(half, tokens_turned, [(0, True, gate_delta)], fresh=1)
    parts = [(0, False, gate_other), (1, True, up_delta)]
    gate_grad, up_grad = up_outer(half, tokens_turned, parts, gate_grad, fresh=1)
    (up_grad,) = up_outer(half, tokens_turned, [(0, False, up_other)], up_grad)
    return (input_grad, gate_grad, up_grad, down_grad)


def whole(sizes, *arrays):
    return per_device(sizes, *arrays)


def solution(mesh):
    sizes = (mesh.shape["row"], mesh.shape["col"])
    return jax.shard_map(
        functools.partial(whole, sizes),
        mesh=mesh,
        in_specs=(
            P("row", "col"),
            P("row", "col"),
            P("col", "row"),
            P("col", "row"),
            P("row", "col"),
        ),
        out_specs=(P("row", "col"), P("col", "row"), P("col", "row"), P("row", "col")),
        check_vma=False,
    )
```

profile of v0, /device:TPU:0, one launch (start us, length us, event | category | flops | bytes accessed | tf_op | source)
XLA Modules:
  0.0 99.5 jit_solution(1465363751243799702)
XLA Ops:
  0.6 4.1 %collective-permute-start = (bf16[16,2048]{1,0:T(8,128)(2,1)}, bf16[16,2048]{1,0:T(8,128)(2,1)S(1)}, u32[]{:S(2)}, u32[]{:S(2)}) collective-permute-start(bf16[16,2048]{1,0:T(8,128)(2,1)} %refs_0_.3), channel_id=1, source_target_pairs={{0,16},{4,20},{8,24},{12,28},{16,0},{20,4},{24,8},{28,12},{1,17},{... | collective-permute-start | bytes 196616 | tf_op jit(solution)/shard_map/ppermute | solution.py:30
  4.8 1.6 %collective-permute-start.1 = (bf16[16,2048]{1,0:T(8,128)(2,1)}, bf16[16,2048]{1,0:T(8,128)(2,1)S(1)}, u32[]{:S(2)}, u32[]{:S(2)}) collective-permute-start(bf16[16,2048]{1,0:T(8,128)(2,1)} %refs_0_.3), channel_id=1, source_target_pairs={{0,8},{4,12},{8,0},{12,4},{16,24},{20,28},{24,16},{28,20},{1,9},{5... | collective-permute-start | bytes 196616 | tf_op jit(solution)/shard_map/ppermute | solution.py:30
  6.3 1.5 %collective-permute-start.3 = (bf16[16,2048]{1,0:T(8,128)(2,1)}, bf16[16,2048]{1,0:T(8,128)(2,1)S(1)}, u32[]{:S(2)}, u32[]{:S(2)}) collective-permute-start(bf16[16,2048]{1,0:T(8,128)(2,1)} %refs_0_.3), channel_id=1, source_target_pairs={{0,4},{4,0},{8,12},{12,8},{16,20},{20,16},{24,28},{28,24},{1,5},{5... | collective-permute-start | bytes 196616 | tf_op jit(solution)/shard_map/ppermute | solution.py:30
  7.9 0.3 collective-permute-start.10
  8.2 0.9 copy-done.7
  9.1 0.8 copy-done.8
  9.9 0.2 shard_map.84
  10.1 2.2 %shard_map.85.refs_7_.top_ref = bf16[1024,2048]{1,0:T(8,128)(2,1)S(1)} custom-call(bf16[2048,2048]{1,0:T(8,128)(2,1)} %refs_0_.5), custom_call_target="tpu_custom_call" | custom-call | bytes 4194304 | tf_op jit(solution)/shard_map/pallas_call | solution.py:86
  12.3 0.0 copy-start
  12.3 2.0 %copy-done = bf16[1024,2048]{1,0:T(8,128)(2,1)} copy-done((bf16[1024,2048]{1,0:T(8,128)(2,1)}, bf16[1024,2048]{1,0:T(8,128)(2,1)S(1)}, u32[]{:S(2)}) %copy-start) | copy-done | bytes 4194328
  14.3 2.2 %shard_map.86.refs_8_.bottom_ref = bf16[1024,2048]{1,0:T(8,128)(2,1)S(1)} custom-call(bf16[2048,2048]{1,0:T(8,128)(2,1)} %refs_0_.5), custom_call_target="tpu_custom_call" | custom-call | bytes 4194304 | tf_op jit(solution)/shard_map/pallas_call | solution.py:86
  16.5 0.0 copy-start.3
  16.5 2.0 %copy-done.3 = bf16[1024,2048]{1,0:T(8,128)(2,1)} copy-done((bf16[1024,2048]{1,0:T(8,128)(2,1)}, bf16[1024,2048]{1,0:T(8,128)(2,1)S(1)}, u32[]{:S(2)}) %copy-start.3) | copy-done | bytes 4194328
  18.5 0.0 collective-permute-done.refs_1_
  18.5 0.0 collective-permute-done.1.refs_2_
  18.6 0.6 collective-permute-start.4
  19.1 0.2 collective-permute-start.2
  19.3 1.9 %collective-permute-start.11 = (bf16[32,2048]{1,0:T(8,128)(2,1)S(1)}, bf16[32,2048]{1,0:T(8,128)(2,1)S(1)}, u32[]{:S(2)}, u32[]{:S(2)}) collective-permute-start(bf16[32,2048]{1,0:T(8,128)(2,1)S(1)} %pad_maximum_fusion.2), channel_id=1, source_target_pairs={{0,8},{4,12},{8,0},{12,4},{16,24},{20,28},{24,16},{28,20},{1,9},{5... | collective-permute-start | bytes 393224 | tf_op jit(solution)/shard_map/ppermute | solution.py:30
  21.2 2.2 %collective-permute-done.2.refs_3_ = bf16[16,2048]{1,0:T(8,128)(2,1)S(1)} collective-permute-done((bf16[16,2048]{1,0:T(8,128)(2,1)S(1)}, bf16[16,2048]{1,0:T(8,128)(2,1)S(1)}, u32[]{:S(2)}, u32[]{:S(2)}) %collective-permute-start.2) | collective-permute-done | bytes 65568 | tf_op jit(solution)/shard_map/ppermute | solution.py:30
  23.4 1.5 %collective-permute-start.5 = (bf16[16,2048]{1,0:T(8,128)(2,1)S(1)}, bf16[16,2048]{1,0:T(8,128)(2,1)S(1)}, u32[]{:S(2)}, u32[]{:S(2)}) collective-permute-start(bf16[16,2048]{1,0:T(8,128)(2,1)S(1)} %collective-permute-done.2.refs_3_), channel_id=1, source_target_pairs={{0,4},{4,0},{8,12},{12,8},{16,20},{20,16},{24,28},{28,24},{1,5},{5... | collective-permute-start | bytes 196616 | tf_op jit(solution)/shard_map/ppermute | solution.py:30
  24.9 2.7 %collective-permute-done.5.refs_6_ = bf16[16,2048]{1,0:T(8,128)(2,1)S(1)} collective-permute-done((bf16[16,2048]{1,0:T(8,128)(2,1)S(1)}, bf16[16,2048]{1,0:T(8,128)(2,1)S(1)}, u32[]{:S(2)}, u32[]{:S(2)}) %collective-permute-start.5) | collective-permute-done | bytes 65568 | tf_op jit(solution)/shard_map/ppermute | solution.py:30
  27.7 2.2 %copy-done.1 = bf16[1024,2048]{1,0:T(8,128)(2,1)S(1)} copy-done((bf16[1024,2048]{1,0:T(8,128)(2,1)S(1)}, bf16[1024,2048]{1,0:T(8,128)(2,1)}, u32[]{:S(2)}) %copy-start.1) | copy-done | bytes 4194328
  29.8 2.2 %copy-done.4 = bf16[1024,2048]{1,0:T(8,128)(2,1)S(1)} copy-done((bf16[1024,2048]{1,0:T(8,128)(2,1)S(1)}, bf16[1024,2048]{1,0:T(8,128)(2,1)}, u32[]{:S(2)}) %copy-start.4) | copy-done | bytes 4194328
  32.0 0.7 shard_map.87
  32.8 0.0 copy-start.6
  32.8 3.7 %copy-done.6 = bf16[2048,2048]{1,0:T(8,128)(2,1)S(1)} copy-done((bf16[2048,2048]{1,0:T(8,128)(2,1)S(1)}, bf16[2048,2048]{1,0:T(8,128)(2,1)}, u32[]{:S(2)}) %copy-start.6) | copy-done | bytes 8388632
  36.5 1.3 %shard_map.89 = (f32[128,1024]{1,0:T(8,128)S(1)}, f32[128,1024]{1,0:T(8,128)S(1)}) custom-call(s32[1]{0:T(128)} %bitcast.half_ref, bf16[128,2048]{1,0:T(8,128)(2,1)S(1)} %get-tuple-element.19.tokens_ref.turn_ref, bf16[2048,2048]{1,0:T(8,128)(2,1)S(1)} %copy-done.6), custom_call_target="tpu_custom_call" | custom-call | flops 1073741824 | bytes 9961472 | tf_op jit(solution)/shard_map/pallas_call | solution.py:126
  37.8 0.1 collective-permute-start.8
  37.9 0.5 collective-permute-start.6
  38.4 0.0 slice-start.3
  38.4 1.6 %collective-permute-start.12 = (bf16[64,2048]{1,0:T(8,128)(2,1)S(1)}, bf16[64,2048]{1,0:T(8,128)(2,1)S(1)}, u32[]{:S(2)}, u32[]{:S(2)}) collective-permute-start(bf16[64,2048]{1,0:T(8,128)(2,1)S(1)} %pad_maximum_fusion), channel_id=1, source_target_pairs={{0,4},{4,0},{8,12},{12,8},{16,20},{20,16},{24,28},{28,24},{1,5},{5... | collective-permute-start | bytes 786440 | tf_op jit(solution)/shard_map/ppermute | solution.py:30
  40.0 0.7 shard_map.88
  40.8 6.0 %collective-permute-done.12 = bf16[64,2048]{1,0:T(8,128)(2,1)S(1)} collective-permute-done((bf16[64,2048]{1,0:T(8,128)(2,1)S(1)}, bf16[64,2048]{1,0:T(8,128)(2,1)S(1)}, u32[]{:S(2)}, u32[]{:S(2)}) %collective-permute-start.12) | collective-permute-done | bytes 262176 | tf_op jit(solution)/shard_map/ppermute | solution.py:30
  46.9 0.0 slice-start
  46.9 2.4 %shard_map.90 = (f32[128,1024]{1,0:T(8,128)S(1)}, f32[128,1024]{1,0:T(8,128)S(1)}, bf16[2048,128]{1,0:T(8,128)(2,1)S(1)}) custom-call(s32[1]{0:T(128)} %bitcast.half_ref, bf16[128,2048]{1,0:T(8,128)(2,1)S(1)} %constant_dynamic-update-slice_fusion.tokens_ref.grads_ref, bf16[2048,2048]{1,0:T(8,128)(2,1)S(1)} %bitcast.4, ...), custom_call_target="tpu_custom_call" | custom-call | flops 1073741824 | bytes 9961472 | tf_op jit(solution)/shard_map/pallas_call | solution.py:126
  49.3 0.1 collective-permute-start.13
  49.4 0.0 slice-start.1
  49.4 0.1 fusion.4
  49.5 1.6 %collective-permute-start.9 = (bf16[128,1024]{1,0:T(8,128)(2,1)S(1)}, bf16[128,1024]{1,0:T(8,128)(2,1)S(1)}, u32[]{:S(2)}, u32[]{:S(2)}) collective-permute-start(bf16[128,1024]{1,0:T(8,128)(2,1)S(1)} %get-tuple-element.37), channel_id=1, source_target_pairs={{0,2},{1,3},{2,0},{3,1},{4,6},{5,7},{6,4},{7,5},{8,10},{9,11},{10,... | collective-permute-start | bytes 786440 | tf_op jit(solution)/shard_map/ppermute | solution.py:30
  51.0 0.1 fusion.5
  51.1 0.6 collective-permute-start.7
  51.7 0.1 fusion.3
  51.8 1.6 %collective-permute-start.14 = (bf16[128,1024]{1,0:T(8,128)(2,1)S(1)}, bf16[128,1024]{1,0:T(8,128)(2,1)S(1)}, u32[]{:S(2)}, u32[]{:S(2)}) collective-permute-start(bf16[128,1024]{1,0:T(8,128)(2,1)S(1)} %get-tuple-element.35), channel_id=1, source_target_pairs={{0,2},{1,3},{2,0},{3,1},{4,6},{5,7},{6,4},{7,5},{8,10},{9,11},{10,... | collective-permute-start | bytes 786440 | tf_op jit(solution)/shard_map/ppermute | solution.py:30
  53.3 5.4 %collective-permute-done.9 = bf16[128,1024]{1,0:T(8,128)(2,1)S(1)} collective-permute-done((bf16[128,1024]{1,0:T(8,128)(2,1)S(1)}, bf16[128,1024]{1,0:T(8,128)(2,1)S(1)}, u32[]{:S(2)}, u32[]{:S(2)}) %collective-permute-start.9) | collective-permute-done | bytes 262176 | tf_op jit(solution)/shard_map/ppermute | solution.py:30
  58.7 5.6 %collective-permute-done.7 = bf16[128,1024]{1,0:T(8,128)(2,1)S(1)} collective-permute-done((bf16[128,1024]{1,0:T(8,128)(2,1)S(1)}, bf16[128,1024]{1,0:T(8,128)(2,1)S(1)}, u32[]{:S(2)}, u32[]{:S(2)}) %collective-permute-start.7) | collective-permute-done | bytes 262176 | tf_op jit(solution)/shard_map/ppermute | solution.py:30
  64.3 0.2 multiply_convert_fusion
  64.6 4.9 %collective-permute-done.14 = bf16[128,1024]{1,0:T(8,128)(2,1)S(1)} collective-permute-done((bf16[128,1024]{1,0:T(8,128)(2,1)S(1)}, bf16[128,1024]{1,0:T(8,128)(2,1)S(1)}, u32[]{:S(2)}, u32[]{:S(2)}) %collective-permute-start.14) | collective-permute-done | bytes 262176 | tf_op jit(solution)/shard_map/ppermute | solution.py:30
  69.5 0.1 convert_add_fusion
  69.5 0.3 multiply_convert_fusion.1
  69.8 0.1 collective-permute-start.15
  69.9 0.5 collective-permute-start.16
  70.4 2.4 %shard_map.91.rest_0_ = f32[128,2048]{1,0:T(8,128)S(1)} custom-call(s32[1]{0:T(128)} %bitcast.half_ref, bf16[128,1024]{1,0:T(8,128)(2,1)S(1)} %get-tuple-element.42.gate_ref.refs_0_, bf16[128,1024]{1,0:T(8,128)(2,1)S(1)} %get-tuple-element.41.up_ref.refs_1_, bf16[1024,2048]{1,0:T(8,128)(2,1)S(1)} %copy-done.2, bf16[1024,2048]{1,0:T(8,128)(2,1)S(1)} %copy-done.5, ...), custom_call_target="tpu_custom_call" | custom-call | flops 1073741824 | bytes 18350080 | tf_op jit(solution)/shard_map/pallas_call | solution.py:154
  72.9 2.4 %shard_map.92 = f32[128,2048]{1,0:T(8,128)S(1)} custom-call(s32[1]{0:T(128)S(6)} %sub.7.half_ref, bf16[128,1024]{1,0:T(8,128)(2,1)S(1)} %collective-permute-done.15.gate_ref.refs_0_, bf16[128,1024]{1,0:T(8,128)(2,1)S(1)} %collective-permute-done.16.up_ref.refs_0_, bf16[1024,2048]{1,0:T(8,128)(2,1)S(1)} %copy-done.2, bf16[1024,2048]{1,0:T(8,128)(2,1)S(1)} %copy-done.5, ...), custom_call_target="tpu_custom_call" | custom-call | flops 1073741824 | bytes 19398656 | tf_op jit(solution)/shard_map/pallas_call | solution.py:154
  75.3 0.1 convert.7
  75.4 1.6 %collective-permute-start.18 = (bf16[32,2048]{1,0:T(8,128)(2,1)S(1)}, bf16[32,2048]{1,0:T(8,128)(2,1)S(1)}, u32[]{:S(2)}, u32[]{:S(2)}) collective-permute-start(bf16[32,2048]{1,0:T(8,128)(2,1)S(1)} %get-tuple-element.44), channel_id=1, source_target_pairs={{0,4},{4,0},{8,12},{12,8},{16,20},{20,16},{24,28},{28,24},{1,5},{5... | collective-permute-start | bytes 393224 | tf_op jit(solution)/shard_map/ppermute | solution.py:30
  77.0 0.5 collective-permute-start.17
  77.5 4.3 %collective-permute-done.18 = bf16[32,2048]{1,0:T(8,128)(2,1)S(1)} collective-permute-done((bf16[32,2048]{1,0:T(8,128)(2,1)S(1)}, bf16[32,2048]{1,0:T(8,128)(2,1)S(1)}, u32[]{:S(2)}, u32[]{:S(2)}) %collective-permute-start.18) | collective-permute-done | bytes 131104 | tf_op jit(solution)/shard_map/ppermute | solution.py:30
  81.8 0.8 collective-permute-start.19
  82.6 4.5 %shard_map.96 = bf16[2048,2048]{1,0:T(8,128)(2,1)} custom-call(s32[1]{0:T(128)} %bitcast.half_ref, bf16[128,1024]{1,0:T(8,128)(2,1)S(1)} %get-tuple-element.32.own_ref, bf16[128,1024]{1,0:T(8,128)(2,1)S(1)} %collective-permute-done.21.other_ref, bf16[128,2048]{1,0:T(8,128)(2,1)S(1)} %constant_dynamic-update-slice_fusion.tokens_ref.grads_ref), custom_call_target="tpu_custom_call" | custom-call | flops 1073741824 | bytes 9437184 | tf_op jit(solution)/shard_map/pallas_call | solution.py:197
  87.1 2.5 %shard_map.93.refs_2_ = bf16[2048,2048]{1,0:T(8,128)(2,1)} custom-call(s32[1]{0:T(128)} %bitcast.half_ref, bf16[2048,128]{1,0:T(8,128)(2,1)S(1)} %get-tuple-element.29.turned_ref, bf16[128,1024]{1,0:T(8,128)(2,1)S(1)} %get-tuple-element.42.gate_ref.refs_0_), custom_call_target="tpu_custom_call" | custom-call | flops 536870912 | bytes 1048576 | tf_op jit(solution)/shard_map/pallas_call | solution.py:232
  89.7 2.6 %collective-permute-start.20 = (bf16[16,2048]{1,0:T(8,128)(2,1)S(1)}, bf16[16,2048]{1,0:T(8,128)(2,1)S(1)}, u32[]{:S(2)}, u32[]{:S(2)}) collective-permute-start(bf16[16,2048]{1,0:T(8,128)(2,1)S(1)} %slice.43), channel_id=1, source_target_pairs={{0,16},{4,20},{8,24},{12,28},{16,0},{20,4},{24,8},{28,12},{1,17},{... | collective-permute-start | bytes 196616 | tf_op jit(solution)/shard_map/ppermute | solution.py:30
  92.3 4.1 %shard_map.94 = (bf16[2048,2048]{1,0:T(8,128)(2,1)}, bf16[2048,2048]{1,0:T(8,128)(2,1)}) custom-call(s32[1]{0:T(128)} %bitcast.half_ref, bf16[2048,128]{1,0:T(8,128)(2,1)S(1)} %get-tuple-element.29.turned_ref, bf16[128,1024]{1,0:T(8,128)(2,1)S(1)} %collective-permute-done.15.gate_ref.refs_0_, ...), custom_call_target="tpu_custom_call", output_to_operand_aliasing={{0}: (4, {})} | custom-call | flops 1073741824 | bytes 1572864 | tf_op jit(solution)/shard_map/pallas_call | solution.py:232
  96.4 2.5 %shard_map.95 = bf16[2048,2048]{1,0:T(8,128)(2,1)} custom-call(s32[1]{0:T(128)} %bitcast.half_ref, bf16[2048,128]{1,0:T(8,128)(2,1)S(1)} %get-tuple-element.29.turned_ref, bf16[128,1024]{1,0:T(8,128)(2,1)S(1)} %collective-permute-done.16.up_ref.refs_0_, bf16[2048,2048]{1,0:T(8,128)(2,1)} %get-tuple-element.31.refs_1_), custom_call_target="tpu_custom_call", output_to_operand_aliasing={{}: (3, {})} | custom-call | flops 536870912 | bytes 1048576 | tf_op jit(solution)/shard_map/pallas_call | solution.py:232
  98.9 0.6 fusion.2
  (40 shorter events, 0.2 us)
Async XLA Ops:
  0.6 17.9 %collective-permute-start = (bf16[16,2048]{1,0:T(8,128)(2,1)}, bf16[16,2048]{1,0:T(8,128)(2,1)S(1)}, u32[]{:S(2)}, u32[]{:S(2)}) collective-permute-start(bf16[16,2048]{1,0:T(8,128)(2,1)} %refs_0_.3), channel_id=1, source_target_pairs={{0,16},{4,20},{8,24},{12,28},{16,0},{20,4},{24,8},{28,12},{1,17},{... | collective-permute-start | bytes 196616 | tf_op jit(solution)/shard_map/ppermute | solution.py:30
  4.8 13.8 %collective-permute-start.1 = (bf16[16,2048]{1,0:T(8,128)(2,1)}, bf16[16,2048]{1,0:T(8,128)(2,1)S(1)}, u32[]{:S(2)}, u32[]{:S(2)}) collective-permute-start(bf16[16,2048]{1,0:T(8,128)(2,1)} %refs_0_.3), channel_id=1, source_target_pairs={{0,8},{4,12},{8,0},{12,4},{16,24},{20,28},{24,16},{28,20},{1,9},{5... | collective-permute-start | bytes 196616 | tf_op jit(solution)/shard_map/ppermute | solution.py:30
  6.3 18.6 %collective-permute-start.3 = (bf16[16,2048]{1,0:T(8,128)(2,1)}, bf16[16,2048]{1,0:T(8,128)(2,1)S(1)}, u32[]{:S(2)}, u32[]{:S(2)}) collective-permute-start(bf16[16,2048]{1,0:T(8,128)(2,1)} %refs_0_.3), channel_id=1, source_target_pairs={{0,4},{4,0},{8,12},{12,8},{16,20},{20,16},{24,28},{28,24},{1,5},{5... | collective-permute-start | bytes 196616 | tf_op jit(solution)/shard_map/ppermute | solution.py:30
  7.9 11.5 %collective-permute-start.10 = (bf16[16,2048]{1,0:T(8,128)(2,1)}, bf16[16,2048]{1,0:T(8,128)(2,1)S(1)}, u32[]{:S(2)}, u32[]{:S(2)}) collective-permute-start(bf16[16,2048]{1,0:T(8,128)(2,1)} %refs_1_.1), channel_id=1, source_target_pairs={{0,16},{4,20},{8,24},{12,28},{16,0},{20,4},{24,8},{28,12},{1,17},{... | collective-permute-start | bytes 196616 | tf_op jit(solution)/shard_map/ppermute | solution.py:30
  8.2 0.9 copy-start.7
  9.1 0.8 copy-start.8
  12.3 2.0 %copy-start = (bf16[1024,2048]{1,0:T(8,128)(2,1)}, bf16[1024,2048]{1,0:T(8,128)(2,1)S(1)}, u32[]{:S(2)}) copy-start(bf16[1024,2048]{1,0:T(8,128)(2,1)S(1)} %shard_map.85.refs_7_.top_ref) | copy-start | bytes 12582916
  16.5 2.0 %copy-start.3 = (bf16[1024,2048]{1,0:T(8,128)(2,1)}, bf16[1024,2048]{1,0:T(8,128)(2,1)S(1)}, u32[]{:S(2)}) copy-start(bf16[1024,2048]{1,0:T(8,128)(2,1)S(1)} %shard_map.86.refs_8_.bottom_ref) | copy-start | bytes 12582916
  18.6 6.4 %collective-permute-start.4 = (bf16[32,2048]{1,0:T(8,128)(2,1)S(1)}, bf16[32,2048]{1,0:T(8,128)(2,1)S(1)}, u32[]{:S(2)}, u32[]{:S(2)}) collective-permute-start(bf16[32,2048]{1,0:T(8,128)(2,1)S(1)} %pad_maximum_fusion.1), channel_id=1, source_target_pairs={{0,4},{4,0},{8,12},{12,8},{16,20},{20,16},{24,28},{28,24},{1,5},{5... | collective-permute-start | bytes 393224 | tf_op jit(solution)/shard_map/ppermute | solution.py:30
  19.1 4.3 %collective-permute-start.2 = (bf16[16,2048]{1,0:T(8,128)(2,1)S(1)}, bf16[16,2048]{1,0:T(8,128)(2,1)S(1)}, u32[]{:S(2)}, u32[]{:S(2)}) collective-permute-start(bf16[16,2048]{1,0:T(8,128)(2,1)S(1)} %collective-permute-done.refs_1_), channel_id=1, source_target_pairs={{0,8},{4,12},{8,0},{12,4},{16,24},{20,28},{24,16},{28,20},{1,9},{5... | collective-permute-start | bytes 196616 | tf_op jit(solution)/shard_map/ppermute | solution.py:30
  19.3 19.1 %collective-permute-start.11 = (bf16[32,2048]{1,0:T(8,128)(2,1)S(1)}, bf16[32,2048]{1,0:T(8,128)(2,1)S(1)}, u32[]{:S(2)}, u32[]{:S(2)}) collective-permute-start(bf16[32,2048]{1,0:T(8,128)(2,1)S(1)} %pad_maximum_fusion.2), channel_id=1, source_target_pairs={{0,8},{4,12},{8,0},{12,4},{16,24},{20,28},{24,16},{28,20},{1,9},{5... | collective-permute-start | bytes 393224 | tf_op jit(solution)/shard_map/ppermute | solution.py:30
  23.4 4.3 %collective-permute-start.5 = (bf16[16,2048]{1,0:T(8,128)(2,1)S(1)}, bf16[16,2048]{1,0:T(8,128)(2,1)S(1)}, u32[]{:S(2)}, u32[]{:S(2)}) collective-permute-start(bf16[16,2048]{1,0:T(8,128)(2,1)S(1)} %collective-permute-done.2.refs_3_), channel_id=1, source_target_pairs={{0,4},{4,0},{8,12},{12,8},{16,20},{20,16},{24,28},{28,24},{1,5},{5... | collective-permute-start | bytes 196616 | tf_op jit(solution)/shard_map/ppermute | solution.py:30
  27.7 2.2 %copy-start.1 = (bf16[1024,2048]{1,0:T(8,128)(2,1)S(1)}, bf16[1024,2048]{1,0:T(8,128)(2,1)}, u32[]{:S(2)}) copy-start(bf16[1024,2048]{1,0:T(8,128)(2,1)} %copy-done) | copy-start | bytes 12582916
  29.8 2.2 %copy-start.4 = (bf16[1024,2048]{1,0:T(8,128)(2,1)S(1)}, bf16[1024,2048]{1,0:T(8,128)(2,1)}, u32[]{:S(2)}) copy-start(bf16[1024,2048]{1,0:T(8,128)(2,1)} %copy-done.3) | copy-start | bytes 12582916
  32.0 8.0 %copy-start.2 = (bf16[1024,2048]{1,0:T(8,128)(2,1)S(1)}, bf16[1024,2048]{1,0:T(8,128)(2,1)}, u32[]{:S(2)}) copy-start(bf16[1024,2048]{1,0:T(8,128)(2,1)} %copy-done) | copy-start | bytes 12582916
  32.0 8.0 %copy-start.5 = (bf16[1024,2048]{1,0:T(8,128)(2,1)S(1)}, bf16[1024,2048]{1,0:T(8,128)(2,1)}, u32[]{:S(2)}) copy-start(bf16[1024,2048]{1,0:T(8,128)(2,1)} %copy-done.3) | copy-start | bytes 12582916
  32.8 3.7 %copy-start.6 = (bf16[2048,2048]{1,0:T(8,128)(2,1)S(1)}, bf16[2048,2048]{1,0:T(8,128)(2,1)}, u32[]{:S(2)}) copy-start(bf16[2048,2048]{1,0:T(8,128)(2,1)} %up_weight_ref.3) | copy-start | bytes 25165828
  36.5 10.3 %slice-start.2 = ((s8[8388608]{0:T(1024)(128)(4,1)}), s8[4194304]{0:T(1024)(128)(4,1)S(1)}, s32[]{:S(2)}) async-start(s8[8388608]{0:T(1024)(128)(4,1)} %bitcast.3), calls=%async_computation.2 | async-start | bytes 8388608
  37.8 11.6 %collective-permute-start.8 = (f32[128,1024]{1,0:T(8,128)S(1)}, f32[128,1024]{1,0:T(8,128)S(1)}, u32[]{:S(2)}, u32[]{:S(2)}) collective-permute-start(f32[128,1024]{1,0:T(8,128)S(1)} %get-tuple-element.22), channel_id=1, source_target_pairs={{0,1},{1,0},{2,3},{3,2},{4,5},{5,4},{6,7},{7,6},{8,9},{9,8},{10,11... | collective-permute-start | bytes 1572872 | tf_op jit(solution)/shard_map/ppermute | solution.py:30
  37.9 13.1 %collective-permute-start.6 = (f32[128,1024]{1,0:T(8,128)S(1)}, f32[128,1024]{1,0:T(8,128)S(1)}, u32[]{:S(2)}, u32[]{:S(2)}) collective-permute-start(f32[128,1024]{1,0:T(8,128)S(1)} %get-tuple-element.20), channel_id=1, source_target_pairs={{0,1},{1,0},{2,3},{3,2},{4,5},{5,4},{6,7},{7,6},{8,9},{9,8},{10,11... | collective-permute-start | bytes 1572872 | tf_op jit(solution)/shard_map/ppermute | solution.py:30
  38.4 8.4 %slice-start.3 = ((s8[8388608]{0:T(1024)(128)(4,1)}), s8[4194304]{0:T(1024)(128)(4,1)S(1)}, s32[]{:S(2)}) async-start(s8[8388608]{0:T(1024)(128)(4,1)} %bitcast.3), calls=%async_computation.3 | async-start | bytes 8388608
  38.4 8.4 %collective-permute-start.12 = (bf16[64,2048]{1,0:T(8,128)(2,1)S(1)}, bf16[64,2048]{1,0:T(8,128)(2,1)S(1)}, u32[]{:S(2)}, u32[]{:S(2)}) collective-permute-start(bf16[64,2048]{1,0:T(8,128)(2,1)S(1)} %pad_maximum_fusion), channel_id=1, source_target_pairs={{0,4},{4,0},{8,12},{12,8},{16,20},{20,16},{24,28},{28,24},{1,5},{5... | collective-permute-start | bytes 786440 | tf_op jit(solution)/shard_map/ppermute | solution.py:30
  46.9 23.5 %slice-start = ((s8[8388608]{0:T(1024)(128)(4,1)}), s8[4194304]{0:T(1024)(128)(4,1)S(1)}, s32[]{:S(2)}) async-start(s8[8388608]{0:T(1024)(128)(4,1)} %bitcast.1), calls=%async_computation | async-start | bytes 8388608
  49.3 2.4 %collective-permute-start.13 = (f32[128,1024]{1,0:T(8,128)S(1)}, f32[128,1024]{1,0:T(8,128)S(1)}, u32[]{:S(2)}, u32[]{:S(2)}) collective-permute-start(f32[128,1024]{1,0:T(8,128)S(1)} %get-tuple-element.25), channel_id=1, source_target_pairs={{0,1},{1,0},{2,3},{3,2},{4,5},{5,4},{6,7},{7,6},{8,9},{9,8},{10,11... | collective-permute-start | bytes 1572872 | tf_op jit(solution)/shard_map/ppermute | solution.py:30
  49.4 21.0 %slice-start.1 = ((s8[8388608]{0:T(1024)(128)(4,1)}), s8[4194304]{0:T(1024)(128)(4,1)S(1)}, s32[]{:S(2)}) async-start(s8[8388608]{0:T(1024)(128)(4,1)} %bitcast.1), calls=%async_computation.1 | async-start | bytes 8388608
  49.5 9.2 %collective-permute-start.9 = (bf16[128,1024]{1,0:T(8,128)(2,1)S(1)}, bf16[128,1024]{1,0:T(8,128)(2,1)S(1)}, u32[]{:S(2)}, u32[]{:S(2)}) collective-permute-start(bf16[128,1024]{1,0:T(8,128)(2,1)S(1)} %get-tuple-element.37), channel_id=1, source_target_pairs={{0,2},{1,3},{2,0},{3,1},{4,6},{5,7},{6,4},{7,5},{8,10},{9,11},{10,... | collective-permute-start | bytes 786440 | tf_op jit(solution)/shard_map/ppermute | solution.py:30
  51.1 13.2 %collective-permute-start.7 = (bf16[128,1024]{1,0:T(8,128)(2,1)S(1)}, bf16[128,1024]{1,0:T(8,128)(2,1)S(1)}, u32[]{:S(2)}, u32[]{:S(2)}) collective-permute-start(bf16[128,1024]{1,0:T(8,128)(2,1)S(1)} %get-tuple-element.39), channel_id=1, source_target_pairs={{0,2},{1,3},{2,0},{3,1},{4,6},{5,7},{6,4},{7,5},{8,10},{9,11},{10,... | collective-permute-start | bytes 786440 | tf_op jit(solution)/shard_map/ppermute | solution.py:30
  51.8 17.7 %collective-permute-start.14 = (bf16[128,1024]{1,0:T(8,128)(2,1)S(1)}, bf16[128,1024]{1,0:T(8,128)(2,1)S(1)}, u32[]{:S(2)}, u32[]{:S(2)}) collective-permute-start(bf16[128,1024]{1,0:T(8,128)(2,1)S(1)} %get-tuple-element.35), channel_id=1, source_target_pairs={{0,2},{1,3},{2,0},{3,1},{4,6},{5,7},{6,4},{7,5},{8,10},{9,11},{10,... | collective-permute-start | bytes 786440 | tf_op jit(solution)/shard_map/ppermute | solution.py:30
  69.8 3.0 %collective-permute-start.15 = (bf16[128,1024]{1,0:T(8,128)(2,1)S(1)}, bf16[128,1024]{1,0:T(8,128)(2,1)S(1)}, u32[]{:S(2)}, u32[]{:S(2)}) collective-permute-start(bf16[128,1024]{1,0:T(8,128)(2,1)S(1)} %get-tuple-element.42.gate_ref.refs_0_), channel_id=1, source_target_pairs={{0,1},{1,0},{2,3},{3,2},{4,5},{5,4},{6,7},{7,6},{8,9},{9,8},{10,11... | collective-permute-start | bytes 786440 | tf_op jit(solution)/shard_map/ppermute | solution.py:30
  69.9 2.9 %collective-permute-start.16 = (bf16[128,1024]{1,0:T(8,128)(2,1)S(1)}, bf16[128,1024]{1,0:T(8,128)(2,1)S(1)}, u32[]{:S(2)}, u32[]{:S(2)}) collective-permute-start(bf16[128,1024]{1,0:T(8,128)(2,1)S(1)} %get-tuple-element.41.up_ref.refs_1_), channel_id=1, source_target_pairs={{0,1},{1,0},{2,3},{3,2},{4,5},{5,4},{6,7},{7,6},{8,9},{9,8},{10,11... | collective-permute-start | bytes 786440 | tf_op jit(solution)/shard_map/ppermute | solution.py:30
  75.4 6.4 %collective-permute-start.18 = (bf16[32,2048]{1,0:T(8,128)(2,1)S(1)}, bf16[32,2048]{1,0:T(8,128)(2,1)S(1)}, u32[]{:S(2)}, u32[]{:S(2)}) collective-permute-start(bf16[32,2048]{1,0:T(8,128)(2,1)S(1)} %get-tuple-element.44), channel_id=1, source_target_pairs={{0,4},{4,0},{8,12},{12,8},{16,20},{20,16},{24,28},{28,24},{1,5},{5... | collective-permute-start | bytes 393224 | tf_op jit(solution)/shard_map/ppermute | solution.py:30
  77.0 5.7 %collective-permute-start.21 = (bf16[128,1024]{1,0:T(8,128)(2,1)S(1)}, bf16[128,1024]{1,0:T(8,128)(2,1)S(1)}, u32[]{:S(2)}, u32[]{:S(2)}) collective-permute-start(bf16[128,1024]{1,0:T(8,128)(2,1)S(1)} %get-tuple-element.32.own_ref), channel_id=1, source_target_pairs={{0,1},{1,0},{2,3},{3,2},{4,5},{5,4},{6,7},{7,6},{8,9},{9,8},{10,11... | collective-permute-start | bytes 786440 | tf_op jit(solution)/shard_map/ppermute | solution.py:30
  77.0 12.6 %collective-permute-start.17 = (bf16[32,2048]{1,0:T(8,128)(2,1)S(1)}, bf16[32,2048]{1,0:T(8,128)(2,1)S(1)}, u32[]{:S(2)}, u32[]{:S(2)}) collective-permute-start(bf16[32,2048]{1,0:T(8,128)(2,1)S(1)} %get-tuple-element.43), channel_id=1, source_target_pairs={{0,4},{4,0},{8,12},{12,8},{16,20},{20,16},{24,28},{28,24},{1,5},{5... | collective-permute-start | bytes 393224 | tf_op jit(solution)/shard_map/ppermute | solution.py:30
  81.8 7.8 %collective-permute-start.19 = (bf16[32,2048]{1,0:T(8,128)(2,1)S(1)}, bf16[32,2048]{1,0:T(8,128)(2,1)S(1)}, u32[]{:S(2)}, u32[]{:S(2)}) collective-permute-start(bf16[32,2048]{1,0:T(8,128)(2,1)S(1)} %fusion), channel_id=1, source_target_pairs={{0,8},{4,12},{8,0},{12,4},{16,24},{20,28},{24,16},{28,20},{1,9},{5... | collective-permute-start | bytes 393224 | tf_op jit(solution)/shard_map/ppermute | solution.py:30
  89.7 9.2 %collective-permute-start.20 = (bf16[16,2048]{1,0:T(8,128)(2,1)S(1)}, bf16[16,2048]{1,0:T(8,128)(2,1)S(1)}, u32[]{:S(2)}, u32[]{:S(2)}) collective-permute-start(bf16[16,2048]{1,0:T(8,128)(2,1)S(1)} %slice.43), channel_id=1, source_target_pairs={{0,16},{4,20},{8,24},{12,28},{16,0},{20,4},{24,8},{28,12},{1,17},{... | collective-permute-start | bytes 196616 | tf_op jit(solution)/shard_map/ppermute | solution.py:30
where the time goes:
time: 99.9 us; the launch traced here: 99.5 us
  waiting for transfers between devices  31.1 us (31%)
  Pallas kernels  28.1 us (28%)
  starting transfers between devices  23.8 us (24%)
  local copies, waits for them, and re-layouts  13.9 us (14%)
  other arithmetic  1.6 us (2%)
  between operations  1 us (1%)
    ppermute x22, waiting for transfers between devices, swap(): return lax.ppermute(value, axis, [(i, i ^ mask) for i in range(size)])  31.1 us
    ppermute x22, starting transfers between devices, swap(): return lax.ppermute(value, axis, [(i, i ^ mask) for i in range(size)])  23.8 us
    unnamed x29, local copies, waits for them, and re-layouts  13.9 us
    pallas_call x3, Pallas kernels, up_outer(): pl.pallas_call(functools.partial(up_kernel, [part[:2] for part in parts],...  9.01 us
    pallas_call x2, Pallas kernels, out_of_hidden(): pl.pallas_call(out_kernel, out_shape=shape, in_specs=[SMEM] + [VMEM] * le...  4.86 us
    pallas_call x3, Pallas kernels, load(): pl.pallas_call(functools.partial(load_kernel, [start for _, start, _ in s...  4.55 us
    pallas_call x1, Pallas kernels, down_outer(): pl.pallas_call(functools.partial(down_kernel, scale), out_shape=shape, in...  4.5 us
    pallas_call x2, Pallas kernels, into_hidden(): pl.pallas_call(kernel, out_shape=(shape, shape, *turned), in_specs=[SMEM,...  3.75 us
  transfers between devices with their start and end apart: 22, of which 7 were waited for; matrix products, arithmetic and copies ran while one was open for 1% of the time, Pallas kernels for 26%

commit v1 on v0

--- a/solution.py
+++ b/solution.py
@@ -142,14 +142,15 @@
             into = pl.ds(part * middle + rows.start, rows.size)
             value = contract_cols(ref[rows, columns], gate_ref[...])
             value += contract_cols(up_weight_ref[into, columns], up_ref[...])
-            value = value.T
             if len(rest) > 1:
-                value += rest[0][:, into]
-            out_ref[:, into] = value
+                out_ref[:, into] = (value + rest[0][into, :]).T
+            else:
+                out_ref[into, :] = value
 
 
 def out_of_hidden(half, gate, up, top, bottom, up_weight, *total):
-    shape = jax.ShapeDtypeStruct((gate.shape[0], up_weight.shape[0]), F32)
+    shape = (gate.shape[0], up_weight.shape[0])
+    shape = jax.ShapeDtypeStruct(shape if total else shape[::-1], F32)
     arrays = [gate, up, top, bottom, up_weight, *total]
     return pl.pallas_call(
         out_kernel,

time: 99.9 us -> 99.7 us (level)
  no operation moved by 1% of the time
where the time goes in v1:
time: 99.7 us; the launch traced here: 99.4 us
  waiting for transfers between devices  31.1 us (31%)
  Pallas kernels  28 us (28%)
  starting transfers between devices  23.8 us (24%)
  local copies, waits for them, and re-layouts  13.9 us (14%)
  other arithmetic  1.6 us (2%)
  between operations  1.01 us (1%)
    ppermute x22, waiting for transfers between devices, swap(): return lax.ppermute(value, axis, [(i, i ^ mask) for i in range(size)])  31.1 us
    ppermute x22, starting transfers between devices, swap(): return lax.ppermute(value, axis, [(i, i ^ mask) for i in range(size)])  23.8 us
    unnamed x29, local copies, waits for them, and re-layouts  13.9 us
    pallas_call x3, Pallas kernels, up_outer(): pl.pallas_call(functools.partial(up_kernel, [part[:2] for part in parts],...  9.01 us
    pallas_call x2, Pallas kernels, out_of_hidden(): pl.pallas_call(out_kernel, out_shape=shape, in_specs=[SMEM] + [VMEM] * le...  4.76 us
    pallas_call x3, Pallas kernels, load(): pl.pallas_call(functools.partial(load_kernel, [start for _, start, _ in s...  4.55 us
    pallas_call x1, Pallas kernels, down_outer(): pl.pallas_call(functools.partial(down_kernel, scale), out_shape=shape, in...  4.43 us
    pallas_call x2, Pallas kernels, into_hidden(): pl.pallas_call(kernel, out_shape=(shape, shape, *turned), in_specs=[SMEM,...  3.75 us
  transfers between devices with their start and end apart: 22, of which 7 were waited for; matrix products, arithmetic and copies ran while one was open for 1% of the time, Pallas kernels for 26%

profile of v1, /device:TPU:0, one launch (start us, length us, event | category | flops | bytes accessed | tf_op | source)
XLA Modules:
  0.0 99.4 jit_solution(13839862928538006123)
XLA Ops:
  0.6 4.1 %collective-permute-start = (bf16[16,2048]{1,0:T(8,128)(2,1)}, bf16[16,2048]{1,0:T(8,128)(2,1)S(1)}, u32[]{:S(2)}, u32[]{:S(2)}) collective-permute-start(bf16[16,2048]{1,0:T(8,128)(2,1)} %refs_0_.3), channel_id=1, source_target_pairs={{0,16},{4,20},{8,24},{12,28},{16,0},{20,4},{24,8},{28,12},{1,17},{... | collective-permute-start | bytes 196616 | tf_op jit(solution)/shard_map/ppermute | solution.py:30
  4.8 1.6 %collective-permute-start.1 = (bf16[16,2048]{1,0:T(8,128)(2,1)}, bf16[16,2048]{1,0:T(8,128)(2,1)S(1)}, u32[]{:S(2)}, u32[]{:S(2)}) collective-permute-start(bf16[16,2048]{1,0:T(8,128)(2,1)} %refs_0_.3), channel_id=1, source_target_pairs={{0,8},{4,12},{8,0},{12,4},{16,24},{20,28},{24,16},{28,20},{1,9},{5... | collective-permute-start | bytes 196616 | tf_op jit(solution)/shard_map/ppermute | solution.py:30
  6.3 1.5 %collective-permute-start.3 = (bf16[16,2048]{1,0:T(8,128)(2,1)}, bf16[16,2048]{1,0:T(8,128)(2,1)S(1)}, u32[]{:S(2)}, u32[]{:S(2)}) collective-permute-start(bf16[16,2048]{1,0:T(8,128)(2,1)} %refs_0_.3), channel_id=1, source_target_pairs={{0,4},{4,0},{8,12},{12,8},{16,20},{20,16},{24,28},{28,24},{1,5},{5... | collective-permute-start | bytes 196616 | tf_op jit(solution)/shard_map/ppermute | solution.py:30
  7.9 0.3 collective-permute-start.10
  8.2 0.9 copy-done.7
  9.1 0.8 copy-done.8
  9.9 0.2 shard_map.84
  10.1 2.2 %shard_map.85.refs_7_.top_ref = bf16[1024,2048]{1,0:T(8,128)(2,1)S(1)} custom-call(bf16[2048,2048]{1,0:T(8,128)(2,1)} %refs_0_.5), custom_call_target="tpu_custom_call" | custom-call | bytes 4194304 | tf_op jit(solution)/shard_map/pallas_call | solution.py:86
  12.3 0.0 copy-start
  12.3 2.0 %copy-done = bf16[1024,2048]{1,0:T(8,128)(2,1)} copy-done((bf16[1024,2048]{1,0:T(8,128)(2,1)}, bf16[1024,2048]{1,0:T(8,128)(2,1)S(1)}, u32[]{:S(2)}) %copy-start) | copy-done | bytes 4194328
  14.3 2.2 %shard_map.86.refs_8_.bottom_ref = bf16[1024,2048]{1,0:T(8,128)(2,1)S(1)} custom-call(bf16[2048,2048]{1,0:T(8,128)(2,1)} %refs_0_.5), custom_call_target="tpu_custom_call" | custom-call | bytes 4194304 | tf_op jit(solution)/shard_map/pallas_call | solution.py:86
  16.5 0.0 copy-start.3
  16.5 2.0 %copy-done.3 = bf16[1024,2048]{1,0:T(8,128)(2,1)} copy-done((bf16[1024,2048]{1,0:T(8,128)(2,1)}, bf16[1024,2048]{1,0:T(8,128)(2,1)S(1)}, u32[]{:S(2)}) %copy-start.3) | copy-done | bytes 4194328
  18.5 0.0 collective-permute-done.refs_1_
  18.5 0.0 collective-permute-done.1.refs_2_
  18.6 0.6 collective-permute-start.4
  19.1 0.2 collective-permute-start.2
  19.3 1.9 %collective-permute-start.11 = (bf16[32,2048]{1,0:T(8,128)(2,1)S(1)}, bf16[32,2048]{1,0:T(8,128)(2,1)S(1)}, u32[]{:S(2)}, u32[]{:S(2)}) collective-permute-start(bf16[32,2048]{1,0:T(8,128)(2,1)S(1)} %pad_maximum_fusion.2), channel_id=1, source_target_pairs={{0,8},{4,12},{8,0},{12,4},{16,24},{20,28},{24,16},{28,20},{1,9},{5... | collective-permute-start | bytes 393224 | tf_op jit(solution)/shard_map/ppermute | solution.py:30
  21.2 2.2 %collective-permute-done.2.refs_3_ = bf16[16,2048]{1,0:T(8,128)(2,1)S(1)} collective-permute-done((bf16[16,2048]{1,0:T(8,128)(2,1)S(1)}, bf16[16,2048]{1,0:T(8,128)(2,1)S(1)}, u32[]{:S(2)}, u32[]{:S(2)}) %collective-permute-start.2) | collective-permute-done | bytes 65568 | tf_op jit(solution)/shard_map/ppermute | solution.py:30
  23.4 1.5 %collective-permute-start.5 = (bf16[16,2048]{1,0:T(8,128)(2,1)S(1)}, bf16[16,2048]{1,0:T(8,128)(2,1)S(1)}, u32[]{:S(2)}, u32[]{:S(2)}) collective-permute-start(bf16[16,2048]{1,0:T(8,128)(2,1)S(1)} %collective-permute-done.2.refs_3_), channel_id=1, source_target_pairs={{0,4},{4,0},{8,12},{12,8},{16,20},{20,16},{24,28},{28,24},{1,5},{5... | collective-permute-start | bytes 196616 | tf_op jit(solution)/shard_map/ppermute | solution.py:30
  24.9 2.7 %collective-permute-done.5.refs_6_ = bf16[16,2048]{1,0:T(8,128)(2,1)S(1)} collective-permute-done((bf16[16,2048]{1,0:T(8,128)(2,1)S(1)}, bf16[16,2048]{1,0:T(8,128)(2,1)S(1)}, u32[]{:S(2)}, u32[]{:S(2)}) %collective-permute-start.5) | collective-permute-done | bytes 65568 | tf_op jit(solution)/shard_map/ppermute | solution.py:30
  27.7 2.2 %copy-done.1 = bf16[1024,2048]{1,0:T(8,128)(2,1)S(1)} copy-done((bf16[1024,2048]{1,0:T(8,128)(2,1)S(1)}, bf16[1024,2048]{1,0:T(8,128)(2,1)}, u32[]{:S(2)}) %copy-start.1) | copy-done | bytes 4194328
  29.8 2.2 %copy-done.4 = bf16[1024,2048]{1,0:T(8,128)(2,1)S(1)} copy-done((bf16[1024,2048]{1,0:T(8,128)(2,1)S(1)}, bf16[1024,2048]{1,0:T(8,128)(2,1)}, u32[]{:S(2)}) %copy-start.4) | copy-done | bytes 4194328
  32.0 0.7 shard_map.87
  32.8 0.0 copy-start.6
  32.8 3.7 %copy-done.6 = bf16[2048,2048]{1,0:T(8,128)(2,1)S(1)} copy-done((bf16[2048,2048]{1,0:T(8,128)(2,1)S(1)}, bf16[2048,2048]{1,0:T(8,128)(2,1)}, u32[]{:S(2)}) %copy-start.6) | copy-done | bytes 8388632
  36.5 1.3 %shard_map.89 = (f32[128,1024]{1,0:T(8,128)S(1)}, f32[128,1024]{1,0:T(8,128)S(1)}) custom-call(s32[1]{0:T(128)} %bitcast.half_ref, bf16[128,2048]{1,0:T(8,128)(2,1)S(1)} %get-tuple-element.19.tokens_ref.turn_ref, bf16[2048,2048]{1,0:T(8,128)(2,1)S(1)} %copy-done.6), custom_call_target="tpu_custom_call" | custom-call | flops 1073741824 | bytes 9961472 | tf_op jit(solution)/shard_map/pallas_call | solution.py:126
  37.8 0.1 collective-permute-start.8
  37.9 0.5 collective-permute-start.6
  38.4 0.0 slice-start.3
  38.4 1.6 %collective-permute-start.12 = (bf16[64,2048]{1,0:T(8,128)(2,1)S(1)}, bf16[64,2048]{1,0:T(8,128)(2,1)S(1)}, u32[]{:S(2)}, u32[]{:S(2)}) collective-permute-start(bf16[64,2048]{1,0:T(8,128)(2,1)S(1)} %pad_maximum_fusion), channel_id=1, source_target_pairs={{0,4},{4,0},{8,12},{12,8},{16,20},{20,16},{24,28},{28,24},{1,5},{5... | collective-permute-start | bytes 786440 | tf_op jit(solution)/shard_map/ppermute | solution.py:30
  40.0 0.7 shard_map.88
  40.8 6.0 %collective-permute-done.12 = bf16[64,2048]{1,0:T(8,128)(2,1)S(1)} collective-permute-done((bf16[64,2048]{1,0:T(8,128)(2,1)S(1)}, bf16[64,2048]{1,0:T(8,128)(2,1)S(1)}, u32[]{:S(2)}, u32[]{:S(2)}) %collective-permute-start.12) | collective-permute-done | bytes 262176 | tf_op jit(solution)/shard_map/ppermute | solution.py:30
  46.9 0.0 slice-start
  46.9 2.4 %shard_map.90 = (f32[128,1024]{1,0:T(8,128)S(1)}, f32[128,1024]{1,0:T(8,128)S(1)}, bf16[2048,128]{1,0:T(8,128)(2,1)S(1)}) custom-call(s32[1]{0:T(128)} %bitcast.half_ref, bf16[128,2048]{1,0:T(8,128)(2,1)S(1)} %constant_dynamic-update-slice_fusion.tokens_ref.grads_ref, bf16[2048,2048]{1,0:T(8,128)(2,1)S(1)} %bitcast.4, ...), custom_call_target="tpu_custom_call" | custom-call | flops 1073741824 | bytes 9961472 | tf_op jit(solution)/shard_map/pallas_call | solution.py:126
  49.3 0.1 collective-permute-start.13
  49.4 0.0 slice-start.1
  49.4 0.1 fusion.4
  49.5 1.6 %collective-permute-start.9 = (bf16[128,1024]{1,0:T(8,128)(2,1)S(1)}, bf16[128,1024]{1,0:T(8,128)(2,1)S(1)}, u32[]{:S(2)}, u32[]{:S(2)}) collective-permute-start(bf16[128,1024]{1,0:T(8,128)(2,1)S(1)} %get-tuple-element.37), channel_id=1, source_target_pairs={{0,2},{1,3},{2,0},{3,1},{4,6},{5,7},{6,4},{7,5},{8,10},{9,11},{10,... | collective-permute-start | bytes 786440 | tf_op jit(solution)/shard_map/ppermute | solution.py:30
  51.0 0.1 fusion.5
  51.1 0.6 collective-permute-start.7
  51.7 0.1 fusion.3
  51.8 1.6 %collective-permute-start.14 = (bf16[128,1024]{1,0:T(8,128)(2,1)S(1)}, bf16[128,1024]{1,0:T(8,128)(2,1)S(1)}, u32[]{:S(2)}, u32[]{:S(2)}) collective-permute-start(bf16[128,1024]{1,0:T(8,128)(2,1)S(1)} %get-tuple-element.35), channel_id=1, source_target_pairs={{0,2},{1,3},{2,0},{3,1},{4,6},{5,7},{6,4},{7,5},{8,10},{9,11},{10,... | collective-permute-start | bytes 786440 | tf_op jit(solution)/shard_map/ppermute | solution.py:30
  53.3 5.4 %collective-permute-done.9 = bf16[128,1024]{1,0:T(8,128)(2,1)S(1)} collective-permute-done((bf16[128,1024]{1,0:T(8,128)(2,1)S(1)}, bf16[128,1024]{1,0:T(8,128)(2,1)S(1)}, u32[]{:S(2)}, u32[]{:S(2)}) %collective-permute-start.9) | collective-permute-done | bytes 262176 | tf_op jit(solution)/shard_map/ppermute | solution.py:30
  58.7 5.6 %collective-permute-done.7 = bf16[128,1024]{1,0:T(8,128)(2,1)S(1)} collective-permute-done((bf16[128,1024]{1,0:T(8,128)(2,1)S(1)}, bf16[128,1024]{1,0:T(8,128)(2,1)S(1)}, u32[]{:S(2)}, u32[]{:S(2)}) %collective-permute-start.7) | collective-permute-done | bytes 262176 | tf_op jit(solution)/shard_map/ppermute | solution.py:30
  64.3 0.2 multiply_convert_fusion
  64.6 4.9 %collective-permute-done.14 = bf16[128,1024]{1,0:T(8,128)(2,1)S(1)} collective-permute-done((bf16[128,1024]{1,0:T(8,128)(2,1)S(1)}, bf16[128,1024]{1,0:T(8,128)(2,1)S(1)}, u32[]{:S(2)}, u32[]{:S(2)}) %collective-permute-start.14) | collective-permute-done | bytes 262176 | tf_op jit(solution)/shard_map/ppermute | solution.py:30
  69.5 0.1 convert_add_fusion
  69.5 0.3 multiply_convert_fusion.1
  69.8 0.1 collective-permute-start.15
  69.9 0.5 collective-permute-start.16
  70.4 2.3 %shard_map.91.rest_0_ = f32[2048,128]{1,0:T(8,128)S(1)} custom-call(s32[1]{0:T(128)} %bitcast.half_ref, bf16[128,1024]{1,0:T(8,128)(2,1)S(1)} %get-tuple-element.42.gate_ref.refs_0_, bf16[128,1024]{1,0:T(8,128)(2,1)S(1)} %get-tuple-element.41.up_ref.refs_1_, bf16[1024,2048]{1,0:T(8,128)(2,1)S(1)} %copy-done.2, bf16[1024,2048]{1,0:T(8,128)(2,1)S(1)} %copy-done.5, ...), custom_call_target="tpu_custom_call" | custom-call | flops 1073741824 | bytes 18350080 | tf_op jit(solution)/shard_map/pallas_call | solution.py:155
  72.7 2.4 %shard_map.92 = f32[128,2048]{1,0:T(8,128)S(1)} custom-call(s32[1]{0:T(128)S(6)} %sub.7.half_ref, bf16[128,1024]{1,0:T(8,128)(2,1)S(1)} %collective-permute-done.15.gate_ref.refs_0_, bf16[128,1024]{1,0:T(8,128)(2,1)S(1)} %collective-permute-done.16.up_ref.refs_0_, bf16[1024,2048]{1,0:T(8,128)(2,1)S(1)} %copy-done.2, bf16[1024,2048]{1,0:T(8,128)(2,1)S(1)} %copy-done.5, ...), custom_call_target="tpu_custom_call" | custom-call | flops 1073741824 | bytes 19398656 | tf_op jit(solution)/shard_map/pallas_call | solution.py:155
  75.2 0.1 convert.7
  75.3 1.6 %collective-permute-start.18 = (bf16[32,2048]{1,0:T(8,128)(2,1)S(1)}, bf16[32,2048]{1,0:T(8,128)(2,1)S(1)}, u32[]{:S(2)}, u32[]{:S(2)}) collective-permute-start(bf16[32,2048]{1,0:T(8,128)(2,1)S(1)} %get-tuple-element.44), channel_id=1, source_target_pairs={{0,4},{4,0},{8,12},{12,8},{16,20},{20,16},{24,28},{28,24},{1,5},{5... | collective-permute-start | bytes 393224 | tf_op jit(solution)/shard_map/ppermute | solution.py:30
  76.9 0.5 collective-permute-start.17
  77.4 4.3 %collective-permute-done.18 = bf16[32,2048]{1,0:T(8,128)(2,1)S(1)} collective-permute-done((bf16[32,2048]{1,0:T(8,128)(2,1)S(1)}, bf16[32,2048]{1,0:T(8,128)(2,1)S(1)}, u32[]{:S(2)}, u32[]{:S(2)}) %collective-permute-start.18) | collective-permute-done | bytes 131104 | tf_op jit(solution)/shard_map/ppermute | solution.py:30
  81.7 0.8 collective-permute-start.19
  82.5 4.4 %shard_map.96 = bf16[2048,2048]{1,0:T(8,128)(2,1)} custom-call(s32[1]{0:T(128)} %bitcast.half_ref, bf16[128,1024]{1,0:T(8,128)(2,1)S(1)} %get-tuple-element.32.own_ref, bf16[128,1024]{1,0:T(8,128)(2,1)S(1)} %collective-permute-done.21.other_ref, bf16[128,2048]{1,0:T(8,128)(2,1)S(1)} %constant_dynamic-update-slice_fusion.tokens_ref.grads_ref), custom_call_target="tpu_custom_call" | custom-call | flops 1073741824 | bytes 9437184 | tf_op jit(solution)/shard_map/pallas_call | solution.py:198
  87.0 2.5 %shard_map.93.refs_2_ = bf16[2048,2048]{1,0:T(8,128)(2,1)} custom-call(s32[1]{0:T(128)} %bitcast.half_ref, bf16[2048,128]{1,0:T(8,128)(2,1)S(1)} %get-tuple-element.29.turned_ref, bf16[128,1024]{1,0:T(8,128)(2,1)S(1)} %get-tuple-element.42.gate_ref.refs_0_), custom_call_target="tpu_custom_call" | custom-call | flops 536870912 | bytes 1048576 | tf_op jit(solution)/shard_map/pallas_call | solution.py:233
  89.5 2.6 %collective-permute-start.20 = (bf16[16,2048]{1,0:T(8,128)(2,1)S(1)}, bf16[16,2048]{1,0:T(8,128)(2,1)S(1)}, u32[]{:S(2)}, u32[]{:S(2)}) collective-permute-start(bf16[16,2048]{1,0:T(8,128)(2,1)S(1)} %slice.43), channel_id=1, source_target_pairs={{0,16},{4,20},{8,24},{12,28},{16,0},{20,4},{24,8},{28,12},{1,17},{... | collective-permute-start | bytes 196616 | tf_op jit(solution)/shard_map/ppermute | solution.py:30
  92.1 4.1 %shard_map.94 = (bf16[2048,2048]{1,0:T(8,128)(2,1)}, bf16[2048,2048]{1,0:T(8,128)(2,1)}) custom-call(s32[1]{0:T(128)} %bitcast.half_ref, bf16[2048,128]{1,0:T(8,128)(2,1)S(1)} %get-tuple-element.29.turned_ref, bf16[128,1024]{1,0:T(8,128)(2,1)S(1)} %collective-permute-done.15.gate_ref.refs_0_, ...), custom_call_target="tpu_custom_call", output_to_operand_aliasing={{0}: (4, {})} | custom-call | flops 1073741824 | bytes 1572864 | tf_op jit(solution)/shard_map/pallas_call | solution.py:233
  96.2 2.5 %shard_map.95 = bf16[2048,2048]{1,0:T(8,128)(2,1)} custom-call(s32[1]{0:T(128)} %bitcast.half_ref, bf16[2048,128]{1,0:T(8,128)(2,1)S(1)} %get-tuple-element.29.turned_ref, bf16[128,1024]{1,0:T(8,128)(2,1)S(1)} %collective-permute-done.16.up_ref.refs_0_, bf16[2048,2048]{1,0:T(8,128)(2,1)} %get-tuple-element.31.refs_1_), custom_call_target="tpu_custom_call", output_to_operand_aliasing={{}: (3, {})} | custom-call | flops 536870912 | bytes 1048576 | tf_op jit(solution)/shard_map/pallas_call | solution.py:233
  98.7 0.6 fusion.2
  (40 shorter events, 0.2 us)
Async XLA Ops:
  0.6 17.9 %collective-permute-start = (bf16[16,2048]{1,0:T(8,128)(2,1)}, bf16[16,2048]{1,0:T(8,128)(2,1)S(1)}, u32[]{:S(2)}, u32[]{:S(2)}) collective-permute-start(bf16[16,2048]{1,0:T(8,128)(2,1)} %refs_0_.3), channel_id=1, source_target_pairs={{0,16},{4,20},{8,24},{12,28},{16,0},{20,4},{24,8},{28,12},{1,17},{... | collective-permute-start | bytes 196616 | tf_op jit(solution)/shard_map/ppermute | solution.py:30
  4.8 13.8 %collective-permute-start.1 = (bf16[16,2048]{1,0:T(8,128)(2,1)}, bf16[16,2048]{1,0:T(8,128)(2,1)S(1)}, u32[]{:S(2)}, u32[]{:S(2)}) collective-permute-start(bf16[16,2048]{1,0:T(8,128)(2,1)} %refs_0_.3), channel_id=1, source_target_pairs={{0,8},{4,12},{8,0},{12,4},{16,24},{20,28},{24,16},{28,20},{1,9},{5... | collective-permute-start | bytes 196616 | tf_op jit(solution)/shard_map/ppermute | solution.py:30
  6.3 18.6 %collective-permute-start.3 = (bf16[16,2048]{1,0:T(8,128)(2,1)}, bf16[16,2048]{1,0:T(8,128)(2,1)S(1)}, u32[]{:S(2)}, u32[]{:S(2)}) collective-permute-start(bf16[16,2048]{1,0:T(8,128)(2,1)} %refs_0_.3), channel_id=1, source_target_pairs={{0,4},{4,0},{8,12},{12,8},{16,20},{20,16},{24,28},{28,24},{1,5},{5... | collective-permute-start | bytes 196616 | tf_op jit(solution)/shard_map/ppermute | solution.py:30
  7.9 11.5 %collective-permute-start.10 = (bf16[16,2048]{1,0:T(8,128)(2,1)}, bf16[16,2048]{1,0:T(8,128)(2,1)S(1)}, u32[]{:S(2)}, u32[]{:S(2)}) collective-permute-start(bf16[16,2048]{1,0:T(8,128)(2,1)} %refs_1_.1), channel_id=1, source_target_pairs={{0,16},{4,20},{8,24},{12,28},{16,0},{20,4},{24,8},{28,12},{1,17},{... | collective-permute-start | bytes 196616 | tf_op jit(solution)/shard_map/ppermute | solution.py:30
  8.2 0.9 copy-start.7
  9.1 0.8 copy-start.8
  12.3 2.0 %copy-start = (bf16[1024,2048]{1,0:T(8,128)(2,1)}, bf16[1024,2048]{1,0:T(8,128)(2,1)S(1)}, u32[]{:S(2)}) copy-start(bf16[1024,2048]{1,0:T(8,128)(2,1)S(1)} %shard_map.85.refs_7_.top_ref) | copy-start | bytes 12582916
  16.5 2.0 %copy-start.3 = (bf16[1024,2048]{1,0:T(8,128)(2,1)}, bf16[1024,2048]{1,0:T(8,128)(2,1)S(1)}, u32[]{:S(2)}) copy-start(bf16[1024,2048]{1,0:T(8,128)(2,1)S(1)} %shard_map.86.refs_8_.bottom_ref) | copy-start | bytes 12582916
  18.6 6.4 %collective-permute-start.4 = (bf16[32,2048]{1,0:T(8,128)(2,1)S(1)}, bf16[32,2048]{1,0:T(8,128)(2,1)S(1)}, u32[]{:S(2)}, u32[]{:S(2)}) collective-permute-start(bf16[32,2048]{1,0:T(8,128)(2,1)S(1)} %pad_maximum_fusion.1), channel_id=1, source_target_pairs={{0,4},{4,0},{8,12},{12,8},{16,20},{20,16},{24,28},{28,24},{1,5},{5... | collective-permute-start | bytes 393224 | tf_op jit(solution)/shard_map/ppermute | solution.py:30
  19.1 4.3 %collective-permute-start.2 = (bf16[16,2048]{1,0:T(8,128)(2,1)S(1)}, bf16[16,2048]{1,0:T(8,128)(2,1)S(1)}, u32[]{:S(2)}, u32[]{:S(2)}) collective-permute-start(bf16[16,2048]{1,0:T(8,128)(2,1)S(1)} %collective-permute-done.refs_1_), channel_id=1, source_target_pairs={{0,8},{4,12},{8,0},{12,4},{16,24},{20,28},{24,16},{28,20},{1,9},{5... | collective-permute-start | bytes 196616 | tf_op jit(solution)/shard_map/ppermute | solution.py:30
  19.3 19.1 %collective-permute-start.11 = (bf16[32,2048]{1,0:T(8,128)(2,1)S(1)}, bf16[32,2048]{1,0:T(8,128)(2,1)S(1)}, u32[]{:S(2)}, u32[]{:S(2)}) collective-permute-start(bf16[32,2048]{1,0:T(8,128)(2,1)S(1)} %pad_maximum_fusion.2), channel_id=1, source_target_pairs={{0,8},{4,12},{8,0},{12,4},{16,24},{20,28},{24,16},{28,20},{1,9},{5... | collective-permute-start | bytes 393224 | tf_op jit(solution)/shard_map/ppermute | solution.py:30
  23.4 4.3 %collective-permute-start.5 = (bf16[16,2048]{1,0:T(8,128)(2,1)S(1)}, bf16[16,2048]{1,0:T(8,128)(2,1)S(1)}, u32[]{:S(2)}, u32[]{:S(2)}) collective-permute-start(bf16[16,2048]{1,0:T(8,128)(2,1)S(1)} %collective-permute-done.2.refs_3_), channel_id=1, source_target_pairs={{0,4},{4,0},{8,12},{12,8},{16,20},{20,16},{24,28},{28,24},{1,5},{5... | collective-permute-start | bytes 196616 | tf_op jit(solution)/shard_map/ppermute | solution.py:30
  27.7 2.2 %copy-start.1 = (bf16[1024,2048]{1,0:T(8,128)(2,1)S(1)}, bf16[1024,2048]{1,0:T(8,128)(2,1)}, u32[]{:S(2)}) copy-start(bf16[1024,2048]{1,0:T(8,128)(2,1)} %copy-done) | copy-start | bytes 12582916
  29.8 2.2 %copy-start.4 = (bf16[1024,2048]{1,0:T(8,128)(2,1)S(1)}, bf16[1024,2048]{1,0:T(8,128)(2,1)}, u32[]{:S(2)}) copy-start(bf16[1024,2048]{1,0:T(8,128)(2,1)} %copy-done.3) | copy-start | bytes 12582916
  32.0 8.0 %copy-start.2 = (bf16[1024,2048]{1,0:T(8,128)(2,1)S(1)}, bf16[1024,2048]{1,0:T(8,128)(2,1)}, u32[]{:S(2)}) copy-start(bf16[1024,2048]{1,0:T(8,128)(2,1)} %copy-done) | copy-start | bytes 12582916
  32.0 8.0 %copy-start.5 = (bf16[1024,2048]{1,0:T(8,128)(2,1)S(1)}, bf16[1024,2048]{1,0:T(8,128)(2,1)}, u32[]{:S(2)}) copy-start(bf16[1024,2048]{1,0:T(8,128)(2,1)} %copy-done.3) | copy-start | bytes 12582916
  32.8 3.7 %copy-start.6 = (bf16[2048,2048]{1,0:T(8,128)(2,1)S(1)}, bf16[2048,2048]{1,0:T(8,128)(2,1)}, u32[]{:S(2)}) copy-start(bf16[2048,2048]{1,0:T(8,128)(2,1)} %up_weight_ref.3) | copy-start | bytes 25165828
  36.5 10.3 %slice-start.2 = ((s8[8388608]{0:T(1024)(128)(4,1)}), s8[4194304]{0:T(1024)(128)(4,1)S(1)}, s32[]{:S(2)}) async-start(s8[8388608]{0:T(1024)(128)(4,1)} %bitcast.3), calls=%async_computation.2 | async-start | bytes 8388608
  37.8 11.6 %collective-permute-start.8 = (f32[128,1024]{1,0:T(8,128)S(1)}, f32[128,1024]{1,0:T(8,128)S(1)}, u32[]{:S(2)}, u32[]{:S(2)}) collective-permute-start(f32[128,1024]{1,0:T(8,128)S(1)} %get-tuple-element.22), channel_id=1, source_target_pairs={{0,1},{1,0},{2,3},{3,2},{4,5},{5,4},{6,7},{7,6},{8,9},{9,8},{10,11... | collective-permute-start | bytes 1572872 | tf_op jit(solution)/shard_map/ppermute | solution.py:30
  37.9 13.1 %collective-permute-start.6 = (f32[128,1024]{1,0:T(8,128)S(1)}, f32[128,1024]{1,0:T(8,128)S(1)}, u32[]{:S(2)}, u32[]{:S(2)}) collective-permute-start(f32[128,1024]{1,0:T(8,128)S(1)} %get-tuple-element.20), channel_id=1, source_target_pairs={{0,1},{1,0},{2,3},{3,2},{4,5},{5,4},{6,7},{7,6},{8,9},{9,8},{10,11... | collective-permute-start | bytes 1572872 | tf_op jit(solution)/shard_map/ppermute | solution.py:30
  38.4 8.4 %slice-start.3 = ((s8[8388608]{0:T(1024)(128)(4,1)}), s8[4194304]{0:T(1024)(128)(4,1)S(1)}, s32[]{:S(2)}) async-start(s8[8388608]{0:T(1024)(128)(4,1)} %bitcast.3), calls=%async_computation.3 | async-start | bytes 8388608
  38.4 8.4 %collective-permute-start.12 = (bf16[64,2048]{1,0:T(8,128)(2,1)S(1)}, bf16[64,2048]{1,0:T(8,128)(2,1)S(1)}, u32[]{:S(2)}, u32[]{:S(2)}) collective-permute-start(bf16[64,2048]{1,0:T(8,128)(2,1)S(1)} %pad_maximum_fusion), channel_id=1, source_target_pairs={{0,4},{4,0},{8,12},{12,8},{16,20},{20,16},{24,28},{28,24},{1,5},{5... | collective-permute-start | bytes 786440 | tf_op jit(solution)/shard_map/ppermute | solution.py:30
  46.9 23.5 %slice-start = ((s8[8388608]{0:T(1024)(128)(4,1)}), s8[4194304]{0:T(1024)(128)(4,1)S(1)}, s32[]{:S(2)}) async-start(s8[8388608]{0:T(1024)(128)(4,1)} %bitcast.1), calls=%async_computation | async-start | bytes 8388608
  49.3 2.4 %collective-permute-start.13 = (f32[128,1024]{1,0:T(8,128)S(1)}, f32[128,1024]{1,0:T(8,128)S(1)}, u32[]{:S(2)}, u32[]{:S(2)}) collective-permute-start(f32[128,1024]{1,0:T(8,128)S(1)} %get-tuple-element.25), channel_id=1, source_target_pairs={{0,1},{1,0},{2,3},{3,2},{4,5},{5,4},{6,7},{7,6},{8,9},{9,8},{10,11... | collective-permute-start | bytes 1572872 | tf_op jit(solution)/shard_map/ppermute | solution.py:30
  49.4 21.0 %slice-start.1 = ((s8[8388608]{0:T(1024)(128)(4,1)}), s8[4194304]{0:T(1024)(128)(4,1)S(1)}, s32[]{:S(2)}) async-start(s8[8388608]{0:T(1024)(128)(4,1)} %bitcast.1), calls=%async_computation.1 | async-start | bytes 8388608
  49.5 9.2 %collective-permute-start.9 = (bf16[128,1024]{1,0:T(8,128)(2,1)S(1)}, bf16[128,1024]{1,0:T(8,128)(2,1)S(1)}, u32[]{:S(2)}, u32[]{:S(2)}) collective-permute-start(bf16[128,1024]{1,0:T(8,128)(2,1)S(1)} %get-tuple-element.37), channel_id=1, source_target_pairs={{0,2},{1,3},{2,0},{3,1},{4,6},{5,7},{6,4},{7,5},{8,10},{9,11},{10,... | collective-permute-start | bytes 786440 | tf_op jit(solution)/shard_map/ppermute | solution.py:30
  51.1 13.2 %collective-permute-start.7 = (bf16[128,1024]{1,0:T(8,128)(2,1)S(1)}, bf16[128,1024]{1,0:T(8,128)(2,1)S(1)}, u32[]{:S(2)}, u32[]{:S(2)}) collective-permute-start(bf16[128,1024]{1,0:T(8,128)(2,1)S(1)} %get-tuple-element.39), channel_id=1, source_target_pairs={{0,2},{1,3},{2,0},{3,1},{4,6},{5,7},{6,4},{7,5},{8,10},{9,11},{10,... | collective-permute-start | bytes 786440 | tf_op jit(solution)/shard_map/ppermute | solution.py:30
  51.8 17.7 %collective-permute-start.14 = (bf16[128,1024]{1,0:T(8,128)(2,1)S(1)}, bf16[128,1024]{1,0:T(8,128)(2,1)S(1)}, u32[]{:S(2)}, u32[]{:S(2)}) collective-permute-start(bf16[128,1024]{1,0:T(8,128)(2,1)S(1)} %get-tuple-element.35), channel_id=1, source_target_pairs={{0,2},{1,3},{2,0},{3,1},{4,6},{5,7},{6,4},{7,5},{8,10},{9,11},{10,... | collective-permute-start | bytes 786440 | tf_op jit(solution)/shard_map/ppermute | solution.py:30
  69.8 2.9 %collective-permute-start.15 = (bf16[128,1024]{1,0:T(8,128)(2,1)S(1)}, bf16[128,1024]{1,0:T(8,128)(2,1)S(1)}, u32[]{:S(2)}, u32[]{:S(2)}) collective-permute-start(bf16[128,1024]{1,0:T(8,128)(2,1)S(1)} %get-tuple-element.42.gate_ref.refs_0_), channel_id=1, source_target_pairs={{0,1},{1,0},{2,3},{3,2},{4,5},{5,4},{6,7},{7,6},{8,9},{9,8},{10,11... | collective-permute-start | bytes 786440 | tf_op jit(solution)/shard_map/ppermute | solution.py:30
  69.9 2.8 %collective-permute-start.16 = (bf16[128,1024]{1,0:T(8,128)(2,1)S(1)}, bf16[128,1024]{1,0:T(8,128)(2,1)S(1)}, u32[]{:S(2)}, u32[]{:S(2)}) collective-permute-start(bf16[128,1024]{1,0:T(8,128)(2,1)S(1)} %get-tuple-element.41.up_ref.refs_1_), channel_id=1, source_target_pairs={{0,1},{1,0},{2,3},{3,2},{4,5},{5,4},{6,7},{7,6},{8,9},{9,8},{10,11... | collective-permute-start | bytes 786440 | tf_op jit(solution)/shard_map/ppermute | solution.py:30
  75.3 6.4 %collective-permute-start.18 = (bf16[32,2048]{1,0:T(8,128)(2,1)S(1)}, bf16[32,2048]{1,0:T(8,128)(2,1)S(1)}, u32[]{:S(2)}, u32[]{:S(2)}) collective-permute-start(bf16[32,2048]{1,0:T(8,128)(2,1)S(1)} %get-tuple-element.44), channel_id=1, source_target_pairs={{0,4},{4,0},{8,12},{12,8},{16,20},{20,16},{24,28},{28,24},{1,5},{5... | collective-permute-start | bytes 393224 | tf_op jit(solution)/shard_map/ppermute | solution.py:30
  76.9 5.7 %collective-permute-start.21 = (bf16[128,1024]{1,0:T(8,128)(2,1)S(1)}, bf16[128,1024]{1,0:T(8,128)(2,1)S(1)}, u32[]{:S(2)}, u32[]{:S(2)}) collective-permute-start(bf16[128,1024]{1,0:T(8,128)(2,1)S(1)} %get-tuple-element.32.own_ref), channel_id=1, source_target_pairs={{0,1},{1,0},{2,3},{3,2},{4,5},{5,4},{6,7},{7,6},{8,9},{9,8},{10,11... | collective-permute-start | bytes 786440 | tf_op jit(solution)/shard_map/ppermute | solution.py:30
  76.9 12.6 %collective-permute-start.17 = (bf16[32,2048]{1,0:T(8,128)(2,1)S(1)}, bf16[32,2048]{1,0:T(8,128)(2,1)S(1)}, u32[]{:S(2)}, u32[]{:S(2)}) collective-permute-start(bf16[32,2048]{1,0:T(8,128)(2,1)S(1)} %get-tuple-element.43), channel_id=1, source_target_pairs={{0,4},{4,0},{8,12},{12,8},{16,20},{20,16},{24,28},{28,24},{1,5},{5... | collective-permute-start | bytes 393224 | tf_op jit(solution)/shard_map/ppermute | solution.py:30
  81.7 7.8 %collective-permute-start.19 = (bf16[32,2048]{1,0:T(8,128)(2,1)S(1)}, bf16[32,2048]{1,0:T(8,128)(2,1)S(1)}, u32[]{:S(2)}, u32[]{:S(2)}) collective-permute-start(bf16[32,2048]{1,0:T(8,128)(2,1)S(1)} %fusion), channel_id=1, source_target_pairs={{0,8},{4,12},{8,0},{12,4},{16,24},{20,28},{24,16},{28,20},{1,9},{5... | collective-permute-start | bytes 393224 | tf_op jit(solution)/shard_map/ppermute | solution.py:30
  89.5 9.2 %collective-permute-start.20 = (bf16[16,2048]{1,0:T(8,128)(2,1)S(1)}, bf16[16,2048]{1,0:T(8,128)(2,1)S(1)}, u32[]{:S(2)}, u32[]{:S(2)}) collective-permute-start(bf16[16,2048]{1,0:T(8,128)(2,1)S(1)} %slice.43), channel_id=1, source_target_pairs={{0,16},{4,20},{8,24},{12,28},{16,0},{20,4},{24,8},{28,12},{1,17},{... | collective-permute-start | bytes 196616 | tf_op jit(solution)/shard_map/ppermute | solution.py:30
